TPU v7x, 32 devices: a whole 2x2x4 slice. The times are simulated.
32 devices in a mesh: groups: 2 (over x), depth: 16 (over z, y, core).
Axes of the slice: x: 2, y: 2, z: 4, core: 2. Of those that a mesh axis runs over, the one named last changes fastest.
Arguments:
- voxels: bfloat16 [256, 32, 16384], P(('groups', 'depth')), parts along dimension 0, may hold values from -6 to 6
- offsets: int32 [256], P('groups'), parts along dimension 0, may hold values from 0 to 127
- w_first: bfloat16 [64, 32], replicated, may hold values from -1 to 1
- decoder_second_weight: bfloat16 [33, 64], replicated, may hold values from -0.75 to 0.75
- cotangent: float32 [32, 32768], P(None, ('groups', 'depth')), parts along dimension 1, may hold values from -6 to 6
Outputs:
- image: float32 [32, 32768], P(None, ('groups', 'depth')), parts along dimension 1
- grad_voxels: bfloat16 [256, 32, 16384], P(('groups', 'depth')), parts along dimension 0
- grad_first: float32 [128, 32], P('groups'), parts along dimension 0
- grad_second: float32 [66, 64], P('groups'), parts along dimension 0
There are 2 independent parts, one for each index of `groups`. A program takes and returns all parts, laid end to end along the dimension named above; an argument that names none is the same for every part. Nothing has to cross between parts.
Inputs may be any that keep to these rules, and one draw needn't show every extreme that they name: offsets[p] counts tiles of 128 rays.
All inputs are finite; a program needn't handle non-finite values.
Results may differ from a plain program's by a relative error of at most 0.0085.
Values may be sent and summed in bfloat16 or wider, within the bound.
A program may use at most 192 MiB of HBM per device.

v0:
```python
import jax
import jax.numpy as jnp
from jax import lax
from jax.sharding import PartitionSpec as P

TILE = 128


def carried_in(x, axis, combine, identity):
    length, position = (lax.axis_size(axis), lax.axis_index(axis))
    everything = jax.tree.map(lambda part: lax.all_gather(part, axis), x)
    start = jax.tree.map(
        lambda part, zero: jnp.broadcast_to(jnp.asarray(zero, part.dtype), part.shape), x, identity
    )

    def step(k, before):
        reached = k < position
        new = combine(before, jax.tree.map(lambda part: part[k], everything))
        return jax.tree.map(lambda a, b: jnp.where(reached, a, b), new, before)

    return lax.fori_loop(0, length, step, start)


def decode_plane(plane, w_first, decoder_second_weight):
    preact = jnp.dot(w_first, plane, preferred_element_type=jnp.float32)
    hidden = jax.nn.silu(preact).astype(jnp.bfloat16)
    output_raw = jnp.dot(decoder_second_weight, hidden, preferred_element_type=jnp.float32)
    return (preact, hidden, output_raw)


def make_slab(output_raw, dscale):
    channels = output_raw.shape[0] - 1
    emitted_light = jax.nn.sigmoid(output_raw[:channels])
    density = jax.nn.softplus(output_raw[channels]) * dscale
    return jnp.concatenate([emitted_light, density[None]], 0).astype(jnp.bfloat16)


def move_rays(values, start):
    doubled = jnp.concatenate([values, values], values.ndim - 1)
    return lax.dynamic_slice_in_dim(doubled, start, values.shape[-1], values.ndim - 1)


def blended_image(slabs, upstream_gradient):
    channels = slabs.shape[1] - 1
    emitted_light = slabs[:, :channels].astype(jnp.float32)
    density = slabs[:, channels].astype(jnp.float32)
    passing = jnp.exp(-density)
    through = jnp.cumprod(passing, axis=0)
    before = jnp.concatenate([jnp.ones_like(through[:1]), through[:-1]], 0)
    sample_weight_rows = before * (1.0 - passing)
    pixel_colour = jnp.einsum("vi,vsi->si", sample_weight_rows, emitted_light)
    objective_value = jnp.einsum("vz,dvz->dz", upstream_gradient, emitted_light)
    running = jnp.cumsum(sample_weight_rows * objective_value, axis=0)
    return (
        passing,
        before,
        sample_weight_rows,
        objective_value,
        running,
        through[-1],
        pixel_colour,
    )


def slab_gradient(
    passing,
    before,
    sample_weight_rows,
    objective_value,
    running,
    upstream_gradient,
    enter,
    prior,
    ray_total,
):
    grad_rad = (enter * sample_weight_rows)[:, None, :] * upstream_gradient[None]
    grad_dens = enter * before * passing * objective_value - (ray_total - (prior + enter * running))
    return jnp.concatenate([grad_rad, grad_dens[:, None, :]], 1).astype(jnp.bfloat16)


def plane_backward(carry, inputs, w_first, decoder_second_weight, dscale):
    plane, grad_sheared, shift_tiles = inputs
    rays_count = plane.shape[1]
    preact, hidden, output_raw = decode_plane(plane, w_first, decoder_second_weight)
    grad_slab = move_rays(grad_sheared, rays_count - TILE * shift_tiles).astype(jnp.float32)
    channels = output_raw.shape[0] - 1
    sig_rad = jax.nn.sigmoid(output_raw[:channels])
    grad_rad = grad_slab[:channels] * sig_rad * (1.0 - sig_rad)
    grad_dens = grad_slab[channels] * dscale * jax.nn.sigmoid(output_raw[channels])
    grad_raw = jnp.concatenate([grad_rad, grad_dens[None]], 0).astype(jnp.bfloat16)
    grad_hidden = jnp.dot(decoder_second_weight.T, grad_raw, preferred_element_type=jnp.float32)
    sig_pre = jax.nn.sigmoid(preact)
    grad_pre = (grad_hidden * sig_pre * (1.0 + preact * (1.0 - sig_pre))).astype(jnp.bfloat16)
    grad_plane = jnp.dot(w_first.T, grad_pre, preferred_element_type=jnp.float32).astype(
        jnp.bfloat16
    )
    contract = (((1,), (1,)), ((), ()))
    acc_first = carry[0] + lax.dot_general(
        grad_pre, plane, contract, preferred_element_type=jnp.float32
    )
    acc_second = carry[1] + lax.dot_general(
        grad_raw, hidden, contract, preferred_element_type=jnp.float32
    )
    return ((acc_first, acc_second), grad_plane)


def join_depth(preceding_samples, later):
    return (preceding_samples[0] * later[0], preceding_samples[1] + preceding_samples[0] * later[1])


def shards(voxels, offsets, w_first, decoder_second_weight, cotangent):
    planes_here = voxels.shape[0]
    rays_count = voxels.shape[2]
    dscale = 3.0 / (planes_here * lax.axis_size("depth"))
    my_offsets = lax.dynamic_slice_in_dim(
        offsets, lax.axis_index("depth") * planes_here, planes_here
    )

    def forward_plane(inputs):
        plane, shift_tiles = inputs
        output_raw = decode_plane(plane, w_first, decoder_second_weight)[2]
        return move_rays(make_slab(output_raw, dscale), TILE * shift_tiles)

    slabs = lax.map(forward_plane, (voxels, my_offsets))
    cotan_full = lax.all_gather(cotangent, "depth", axis=1, tiled=True)
    passing, before, sample_weight_rows, objective_value, running, last_pass, pixel_colour = (
        blended_image(slabs, cotan_full)
    )
    identity = (jnp.ones((rays_count,), jnp.float32), jnp.zeros((rays_count,), jnp.float32))
    enter, prior = carried_in((last_pass, running[-1]), "depth", join_depth, identity)
    image = lax.psum_scatter(
        (enter[None, :] * pixel_colour).astype(jnp.bfloat16),
        "depth",
        scatter_dimension=1,
        tiled=True,
    ).astype(jnp.float32)
    ray_total = lax.psum(enter * running[-1], "depth")
    grad_sheared = slab_gradient(
        passing,
        before,
        sample_weight_rows,
        objective_value,
        running,
        cotan_full,
        enter,
        prior,
        ray_total,
    )

    def step_plane(carry, inputs):
        return plane_backward(carry, inputs, w_first, decoder_second_weight, dscale)

    start = (
        jnp.zeros(w_first.shape, jnp.float32),
        jnp.zeros(decoder_second_weight.shape, jnp.float32),
    )
    grads, grad_voxels = lax.scan(step_plane, start, (voxels, grad_sheared, my_offsets))
    grad_first, grad_second = lax.psum((grads[0], grads[1]), "depth")
    return (image, grad_voxels, grad_first, grad_second)


def solution(mesh):
    placed = (
        P(("groups", "depth"), None, None),
        P("groups"),
        P(),
        P(),
        P(None, ("groups", "depth")),
    )
    return jax.shard_map(
        shards,
        mesh=mesh,
        in_specs=placed,
        out_specs=(
            P(None, ("groups", "depth")),
            P(("groups", "depth"), None, None),
            P("groups", None),
            P("groups", None),
        ),
        check_vma=False,
    )
```

profile of v0, /device:TPU:0, one launch (start us, length us, event | category | flops | bytes accessed | tf_op | source)
XLA Modules:
  0.0 509.5 jit_solution(6826601035161955763)
XLA Ops:
  8.7 59.9 %while.43 = (s32[]{:T(128)}, bf16[8,33,16384]{2,1,0:T(8,128)(2,1)}, bf16[8,32,16384]{2,1,0:T(8,128)(2,1)}, bf16[64,32]{0,1:T(8,128)(2,1)}, bf16[33,64]{1,0:T(8,1...) while((s32[]{:T(128)}, bf16[8,33,16384]{2,1,0:T(8,128)(2,1)}, ...), condition=%wide.region_1.2_spmd, body=%wide.region_0.1_spmd.sunk | while | flops 148111360 | bytes 8865971 | solution.py:124
  9.9 3.1 convolution_bitcast_fusion.7
  13.9 2.3 fusion.82
  17.4 3.1 convolution_bitcast_fusion.7
  21.4 2.3 fusion.82
  24.9 3.1 convolution_bitcast_fusion.7
  28.9 2.3 fusion.82
  32.4 3.1 convolution_bitcast_fusion.7
  36.3 2.3 fusion.82
  39.8 3.1 convolution_bitcast_fusion.7
  43.8 2.3 fusion.82
  47.3 3.1 convolution_bitcast_fusion.7
  51.3 2.3 fusion.82
  54.8 3.1 convolution_bitcast_fusion.7
  58.8 2.3 fusion.82
  62.3 3.1 convolution_bitcast_fusion.7
  66.3 2.2 fusion.82
  68.6 12.2 %copy.12 = bf16[8,33,16384]{2,0,1:T(8,128)(2,1)} copy(bf16[8,33,16384]{2,1,0:T(8,128)(2,1)} %get-tuple-element.261) | data formatting | bytes 17301504 | tf_op jit(solution)/shard_map/while | solution.py:124
  83.3 6.6 %multiply_reduce_fusion.1 = f32[16384,8]{0,1:T(8,128)S(1)} fusion(f32[16384,32]{0,1:T(8,128)} %bitcast.152, bf16[8,33,16384]{2,1,0:T(8,128)(2,1)} %get-tuple-element.261), kind=kLoop, calls=%fused_computation.69 | loop fusion | flops 12451840 | bytes 11010048 | tf_op jit(solution)/shard_map/vz,dvz->dz/dot_general | solution.py:52
  92.2 31.6 %all-gather.8.cloned.1.call-done = f32[16,1,16384]{2,1,0:T(1,128)} async-done(((f32[1,1,16384]{2,1,0:T(1,128)}), f32[16,1,16384]{2,1,0:T(1,128)}) %all-gather.8.cloned.1.call-update) | async-done | bytes 1048592 | tf_op jit(solution)/shard_map/all_gather | solution.py:11
  123.8 1.8 copy.33
  125.6 37.8 %all-gather.10.cloned.1.call-done = f32[16,1,16384]{2,1,0:T(1,128)} async-done(((f32[1,1,16384]{2,1,0:T(1,128)}), f32[16,1,16384]{2,1,0:T(1,128)}) %all-gather.10.cloned.1.call-update) | async-done | bytes 1048592 | tf_op jit(solution)/shard_map/all_gather | solution.py:11
  163.4 2.8 copy.32
  166.2 19.4 %while.44 = (s32[]{:T(128)}, f32[16384]{0:T(1024)S(1)}, f32[16384]{0:T(1024)S(1)}, s32[]{:T(128)}, f32[16,16384]{1,0:T(8,128)S(1)}, /*index=5*/f32[16,16384]{1,0:T(8,128)}, s32[]{:T(128)}, s32[]{:T(128)}) while((s32[]{:T(128)}, f32[16384]{0:T(1024)S(1)}, f32[16384]{0:T(1024)S(1)}, s32[]{:T(128)}, f32[16,16384]{1,0:T(8,128)S(1)}, ...), condition=%wide.region_5.6_spmd.clone, body=%wide.region_4.5_spmd.clone.sunk | while | flops 114692 | bytes 655477 | solution.py:21
  186.3 85.3 %all-reduce.4.cloned.1.call-done = f32[16384]{0:T(1024)} async-done(((f32[16384]{0:T(1024)}), f32[16384]{0:T(1024)}) %all-reduce.4.cloned.1.call-update) | async-done | bytes 65552 | tf_op jit(solution)/shard_map/psum | solution.py:137
  272.8 5.4 %multiply_reduce_fusion = f32[16384,32]{0,1:T(8,128)S(1)} fusion(f32[16384,8]{0,1:T(8,128)S(1)} %get-tuple-element.370, bf16[8,33,16384]{2,1,0:T(8,128)(2,1)} %get-tuple-element.261), kind=kLoop, calls=%fused_computation.68 | loop fusion | flops 12058624 | bytes 11010048 | tf_op jit(solution)/shard_map/vi,vsi->si/dot_general | solution.py:51
  280.2 4.6 multiply_convert_fusion.2
  284.8 9.0 %pad_maximum_fusion.3 = bf16[8,33,16384]{2,1,0:T(8,128)(2,1)} fusion(bf16[8,1,16384]{2,1,0:T(2,128)(2,1)S(1)} %copy.13, bf16[8,32,16384]{2,1,0:T(8,128)(2,1)} %multiply_convert_fusion.2), kind=kLoop, calls=%fused_computation.71 | loop fusion | flops 17301504 | bytes 17301504 | tf_op jit(solution)/shard_map/concatenate | solution.py:78
  293.8 147.4 %while.45 = (s32[]{:T(128)}, f32[64,32]{0,1:T(8,128)S(1)}, f32[33,64]{1,0:T(8,128)S(1)}, bf16[8,32,16384]{2,1,0:T(8,128)(2,1)}, bf16[8,33,16384]{2,1,0:T(8,128)(...) while((s32[]{:T(128)}, f32[64,32]{0,1:T(8,128)S(1)}, ...), condition=%wide.region_9.10_spmd.clone, body=%wide.region_8.9_spmd.clone.sunk | while | flops 434413696 | bytes 81249400 | solution.py:157
  293.8 4.7 multiply_convert_fusion.5
  304.2 1.6 copy-done.7
  305.8 2.0 fusion.95
  307.9 2.1 convolution_add_fusion.4
  312.3 4.7 multiply_convert_fusion.5
  319.5 1.4 dynamic-slice_bitcast_fusion.2
  322.6 1.6 copy-done.7
  324.2 2.0 fusion.95
  326.3 2.1 convolution_add_fusion.4
  330.7 4.7 multiply_convert_fusion.5
  341.0 1.6 copy-done.7
  342.7 2.0 fusion.95
  344.8 2.1 convolution_add_fusion.4
  349.1 4.7 multiply_convert_fusion.5
  359.5 1.6 copy-done.7
  361.1 2.0 fusion.95
  363.2 2.1 convolution_add_fusion.4
  367.5 4.7 multiply_convert_fusion.5
  377.9 1.6 copy-done.7
  379.5 2.0 fusion.95
  381.6 2.1 convolution_add_fusion.4
  386.0 4.7 multiply_convert_fusion.5
  396.3 1.6 copy-done.7
  397.9 2.0 fusion.95
  400.0 2.1 convolution_add_fusion.4
  404.4 4.7 multiply_convert_fusion.5
  414.7 1.6 copy-done.7
  416.3 2.0 fusion.95
  418.4 2.1 convolution_add_fusion.4
  422.8 4.7 multiply_convert_fusion.5
  433.1 1.6 copy-done.7
  434.7 2.0 fusion.95
  436.8 2.1 convolution_add_fusion.4
  441.2 60.3 %all-reduce.1 = (f32[64,32]{0,1:T(8,128)}, f32[33,64]{1,0:T(8,128)}) all-reduce(f32[64,32]{0,1:T(8,128)S(1)} %get-tuple-element.265, f32[33,64]{1,0:T(8,128)S(1)} %get-tuple-element.266), channel_id=1, replica_groups=mesh['groups'=2,'depth'=16] {'depth'}, use_global_device_ids=true, to_apply=%region_10.11 | all-reduce | flops 4160 | bytes 33280 | tf_op jit(solution)/shard_map/psum | solution.py:158
  501.4 1.5 convert_element_type.53
  (226 shorter events, 97.0 us)
Async XLA Ops:
  7.2 76.1 %all-gather.6.cloned.1.call-start = ((), (), s32[]{:S(2)}) async-start(), calls=%async_computation.1 | async-start | bytes 2228224 | tf_op jit(solution)/shard_map/all_gather | solution.py:125
  7.9 115.9 %all-gather.8.cloned.1.call-start = ((), (), s32[]{:S(2)}) async-start(), calls=%async_computation.4 | async-start | bytes 1114112 | tf_op jit(solution)/shard_map/all_gather | solution.py:11
  83.0 80.4 %all-gather.10.cloned.1.call-start = ((), (), s32[]{:S(2)}) async-start(), calls=%async_computation.5 | async-start | bytes 1114112 | tf_op jit(solution)/shard_map/all_gather | solution.py:11
  92.1 179.5 %all-reduce.4.cloned.1.call-start = ((), (), s32[]{:S(2)}) async-start(), calls=%async_computation.3 | async-start | bytes 131072 | tf_op jit(solution)/shard_map/psum | solution.py:137
  186.2 315.2 %reduce-scatter.2.cloned.1.call-start = ((), (), s32[]{:S(2)}) async-start(), calls=%async_computation.2 | async-start | bytes 1114112 | tf_op jit(solution)/shard_map/reduce_scatter | solution.py:131
  278.2 2.0 copy-start.4
  284.8 9.1 %copy-start.5 = (bf16[33,64]{1,0:T(8,128)(2,1)S(1)}, bf16[33,64]{1,0:T(8,128)(2,1)}, u32[]{:S(2)}) copy-start(bf16[33,64]{1,0:T(8,128)(2,1)} %get-tuple-element.627) | copy-start | bytes 12676
  284.8 9.1 %copy-start.6 = (bf16[64,32]{0,1:T(8,128)(2,1)S(1)}, bf16[64,32]{0,1:T(8,128)(2,1)}, u32[]{:S(2)}) copy-start(bf16[64,32]{0,1:T(8,128)(2,1)} %get-tuple-element.628) | copy-start | bytes 12292
  298.6 1.3 copy-start
  303.6 2.2 copy-start.7
  305.8 2.1 copy-start.2
  307.9 2.1 copy-start.3
  307.9 2.2 copy-start.1
  317.0 1.3 copy-start
  322.0 2.2 copy-start.7
  324.2 2.1 copy-start.2
  326.3 2.1 copy-start.3
  326.3 2.2 copy-start.1
  335.4 1.3 copy-start
  340.5 2.2 copy-start.7
  342.7 2.1 copy-start.2
  344.7 2.1 copy-start.3
  344.7 2.2 copy-start.1
  353.8 1.3 copy-start
  358.9 2.2 copy-start.7
  361.1 2.1 copy-start.2
  363.1 2.1 copy-start.3
  363.2 2.2 copy-start.1
  372.3 1.3 copy-start
  377.3 2.2 copy-start.7
  379.5 2.1 copy-start.2
  381.6 2.1 copy-start.3
  381.6 2.2 copy-start.1
  390.7 1.3 copy-start
  395.7 2.2 copy-start.7
  397.9 2.1 copy-start.2
  400.0 2.1 copy-start.3
  400.0 2.2 copy-start.1
  409.1 1.3 copy-start
  414.1 2.2 copy-start.7
  416.3 2.1 copy-start.2
  418.4 2.1 copy-start.3
  418.4 2.2 copy-start.1
  427.5 1.3 copy-start
  432.5 2.2 copy-start.7
  434.7 2.1 copy-start.2
  436.8 2.1 copy-start.3
  436.8 2.2 copy-start.1
Sparse Core Ops, SparseCore 0:
  10.2 44.1 all-gather.5
  83.1 40.6 all-gather.7
  126.5 36.8 all-gather.9
  186.3 85.2 all-reduce.3
  279.5 59.1 reduce-scatter.1
where the time goes:
time: 512 us; the launch traced here: 509 us
  waiting for transfers between devices  155 us (30%)
  matrix products  116 us (23%)
  local copies, waits for them, and re-layouts  79.1 us (15%)
  other arithmetic  72.1 us (14%)
  blocking collectives  60.3 us (12%)
  between operations  13.9 us (3%)
  loops' own time  12 us (2%)
    psum x1, waiting for transfers between devices, shards(): ray_total = lax.psum(enter * running[-1], 'depth')  85.3 us
    all_gather x2, waiting for transfers between devices, carried_in(): everything = jax.tree.map(lambda part: lax.all_gather(part, axis), x)  69.3 us
    psum x1, blocking collectives, shards(): grad_first, grad_second = lax.psum((grads[0], grads[1]), 'depth')  60.3 us
    dot_general x8, matrix products, decode_plane(): preact = jnp.dot(w_first, plane, preferred_element_type=jnp.float32)  37.7 us
    dot_general x16, matrix products, decode_plane(): jnp.dot(decoder_second_weight, hidden, preferred_element_type=jnp.float32)  28.6 us
    while x80, local copies, waits for them, and re-layouts  20.5 us
    dynamic_slice x16, local copies, waits for them, and re-layouts, step(): new = combine(before, jax.tree.map(lambda part: part[k], everything))  18.2 us
    dynamic_update_slice x8, other arithmetic, shards(): slabs = lax.map(forward_plane, (voxels, my_offsets))  18.2 us
  transfers between devices with their start and end apart: 5, of which 3 were waited for; matrix products, arithmetic and copies ran while one was open for 42% of the time, Pallas kernels for 0%

commit v1 on v0

v1 whole, which is shorter than its diff:
```python
import functools

import jax
import jax.numpy as jnp
from jax import lax
from jax.experimental import pallas as pl
from jax.experimental.pallas import tpu as pltpu
from jax.sharding import PartitionSpec as P

TILE = 128
PACK = 4
BF = jnp.bfloat16
F32 = jnp.float32
NT = (((1,), (1,)), ((), ()))


def dot(a, b):
    return jnp.dot(a, b, preferred_element_type=F32)


def running_sum(x):
    rows = x.shape[0]
    row = lax.broadcasted_iota(jnp.int32, x.shape, 0)
    s = 1
    while s < rows:
        x = x + jnp.where(row >= s, pltpu.roll(x, s, 0), 0.0)
        s *= 2
    return x


def gather_tiles(off_ref, vox_ref, x_ref, step):
    planes, feats, rays = vox_ref.shape
    tiles = x_ref.shape[1] // TILE
    total = rays // TILE
    for p in range(planes):
        for j in range(tiles):
            t = lax.rem(step * tiles + j + off_ref[p], total)
            x_ref[pl.ds(p * feats, feats), pl.ds(j * TILE, TILE)] = vox_ref[
                p, :, pl.ds(pl.multiple_of(t * TILE, TILE), TILE)
            ]


def absorb(dens):
    upto = running_sum(dens)
    passing = jnp.exp(-dens)
    before = jnp.exp(dens - upto)
    return upto, passing, before


def softplus(x):
    return jnp.maximum(x, 0.0) + jnp.log1p(jnp.exp(-jnp.abs(x)))


def forward_kernel(dscale, off_ref, vox_ref, w1_ref, w2_ref, col_ref, last_ref, x_ref, rad_ref):
    step = pl.program_id(0)
    gather_tiles(off_ref, vox_ref, x_ref, step)
    halves, rows = w2_ref.shape[0], w2_ref.shape[1]
    planes = vox_ref.shape[0]
    wide = rows - planes
    kin = w1_ref.shape[1]
    raw_d = None
    for h in range(halves):
        half = dot(w1_ref[...], x_ref[pl.ds(h * kin, kin), :])
        hidden = (half + half * jnp.tanh(half)).astype(BF)
        raw = dot(w2_ref[h], hidden)
        rad_ref[pl.ds(h * wide, wide), :] = 0.5 * jnp.tanh(raw[:wide]) + 0.5
        d = raw[wide:]
        raw_d = d if raw_d is None else raw_d + d
    dens = softplus(raw_d) * dscale
    upto, passing, before = absorb(dens)
    weight = before * (1.0 - passing)
    chans = col_ref.shape[1]
    colour = None
    for p in range(planes):
        term = weight[p : p + 1] * rad_ref[pl.ds(p * chans, chans), :]
        colour = term if colour is None else colour + term
    col_ref[0] = colour
    last_ref[0] = jnp.exp(-upto[planes - 1 : planes])


def backward_kernel(
    dscale,
    off_ref,
    vox_ref,
    w1_ref,
    w2_ref,
    w1t_ref,
    w2t_ref,
    ones_ref,
    cot_ref,
    state_ref,
    gvox_ref,
    acc1_ref,
    acc2_ref,
    x_ref,
    half_ref,
    tanh_ref,
    hid_ref,
    slope_ref,
    graw_ref,
    prod_ref,
):
    step = pl.program_id(0)

    @pl.when(step == 0)
    def _():
        acc1_ref[...] = jnp.zeros_like(acc1_ref)
        acc2_ref[...] = jnp.zeros_like(acc2_ref)

    gather_tiles(off_ref, vox_ref, x_ref, step)
    halves, rows = w2_ref.shape[0], w2_ref.shape[1]
    planes, feats, rays = vox_ref.shape
    wide = rows - planes
    kin = w1_ref.shape[1]
    kmid = w1_ref.shape[0]
    chans = cot_ref.shape[1]
    cot = cot_ref[0].astype(F32)
    raw_d = None
    for h in range(halves):
        half = dot(w1_ref[...], x_ref[pl.ds(h * kin, kin), :])
        t = jnp.tanh(half)
        half_ref[pl.ds(h * kmid, kmid), :] = (1.0 + t) * (1.0 + half * (1.0 - t))
        hidden = (half + half * t).astype(BF)
        hid_ref[pl.ds(h * kmid, kmid), :] = hidden
        raw = dot(w2_ref[h], hidden)
        s = jnp.tanh(raw[:wide])
        slope_ref[pl.ds(h * wide, wide), :] = 0.25 - 0.25 * s * s
        for k in range(PACK):
            prod_ref[pl.ds(h * wide + k * chans, chans), :] = (
                cot * (0.5 * s[k * chans : (k + 1) * chans] + 0.5)
            ).astype(BF)
        d = raw[wide:]
        raw_d = d if raw_d is None else raw_d + d
    score = dot(ones_ref[...], prod_ref[...])
    dens = softplus(raw_d) * dscale
    upto, passing, before = absorb(dens)
    enter = state_ref[0, 0:1, :]
    rest = state_ref[0, 1:2, :]
    before = enter * before
    weight = before * (1.0 - passing)
    running = running_sum(weight * score)
    grad_d = before * passing * score - (rest - running)
    grad_d = (grad_d * (dscale * (0.5 * jnp.tanh(0.5 * raw_d) + 0.5))).astype(BF)
    for h in range(halves):
        for k in range(PACK):
            p = h * PACK + k
            graw_ref[h, pl.ds(k * chans, chans), :] = (
                (weight[p : p + 1] * cot) * slope_ref[pl.ds(p * chans, chans), :]
            ).astype(BF)
        graw_ref[h, pl.ds(wide, planes), :] = grad_d
        graw = graw_ref[h]
        ghid = dot(w2t_ref[h], graw)
        gpre = (ghid * half_ref[pl.ds(h * kmid, kmid), :]).astype(BF)
        gx = dot(w1t_ref[...], gpre).astype(BF)
        x = x_ref[pl.ds(h * kin, kin), :]
        acc1_ref[...] += lax.dot_general(gpre, x, NT, preferred_element_type=F32)
        acc2_ref[h] += lax.dot_general(
            graw, hid_ref[pl.ds(h * kmid, kmid), :], NT, preferred_element_type=F32
        )
        tiles = x_ref.shape[1] // TILE
        for k in range(PACK):
            p = h * PACK + k
            for j in range(tiles):
                t = lax.rem(step * tiles + j + off_ref[p], rays // TILE)
                gvox_ref[p, :, pl.ds(pl.multiple_of(t * TILE, TILE), TILE)] = gx[
                    k * feats : (k + 1) * feats, j * TILE : (j + 1) * TILE
                ]


def greet(n, me):
    barrier = pltpu.get_barrier_semaphore()
    for s in range(1, n):
        pl.semaphore_signal(
            barrier,
            inc=1,
            device_id={"depth": lax.rem(me + s, n)},
            device_id_type=pl.DeviceIdType.MESH,
        )
    pl.semaphore_wait(barrier, n - 1)


def swap(n, me, source, target, send_sem, recv_sem):
    copies = []
    for s in range(1, n):
        to = lax.rem(me + s, n)
        copies.append(
            pltpu.make_async_remote_copy(
                src_ref=source(to),
                dst_ref=target.at[me],
                send_sem=send_sem.at[s],
                recv_sem=recv_sem.at[s],
                device_id={"depth": to},
                device_id_type=pl.DeviceIdType.MESH,
            )
        )
    for copy in copies:
        copy.start()
    return copies


def state_kernel(n, last_ref, col_ref, cot_ref, out_ref, mine, got, back, s1, r1, s2, r2):
    me = lax.axis_index("depth")
    greet(n, me)

    def fill(d, carry):
        mine[d, 0:1, :] = last_ref[d]
        mine[d, 1:2, :] = jnp.sum(col_ref[d] * cot_ref[d].astype(F32), axis=0, keepdims=True)
        return carry

    lax.fori_loop(0, n, fill, 0)
    copies = swap(n, me, lambda to: mine.at[to], got, s1, r1)
    got[me] = mine[me]
    for copy in copies:
        copy.wait()
    enter = jnp.ones_like(got[0, 0:1, :])
    prior = jnp.zeros_like(enter)
    for d in range(n):
        back[d, 0:1, :] = enter
        back[d, 1:2, :] = prior
        prior = prior + enter * got[d, 1:2, :]
        enter = enter * got[d, 0:1, :]
    for d in range(n):
        back[d, 1:2, :] = prior - back[d, 1:2, :]
    copies = swap(n, me, lambda to: back.at[to], out_ref, s2, r2)
    out_ref[me] = back[me]
    for copy in copies:
        copy.wait()


def exchange_state(n, last, colour, cot):
    chunk = last.shape[2]
    shape = (n, 2, chunk)
    vmem = pl.BlockSpec(memory_space=pltpu.VMEM)
    return pl.pallas_call(
        functools.partial(state_kernel, n),
        out_shape=jax.ShapeDtypeStruct(shape, F32),
        in_specs=[vmem] * 3,
        out_specs=vmem,
        scratch_shapes=[pltpu.VMEM(shape, F32)] * 3 + [pltpu.SemaphoreType.DMA((n,))] * 4,
        compiler_params=pltpu.CompilerParams(collective_id=1, has_side_effects=True),
        name="exchange_state",
    )(last, colour, cot)


def total_kernel(n, in_ref, out_ref, got, mine, s1, r1, s2, r2):
    me = lax.axis_index("depth")
    greet(n, me)
    copies = swap(n, me, lambda to: in_ref.at[to], got, s1, r1)
    got[me] = in_ref[me]
    for copy in copies:
        copy.wait()
    mine[...] = jnp.sum(got[...], axis=0)
    copies = swap(n, me, lambda to: mine, out_ref, s2, r2)
    out_ref[me] = mine[...]
    for copy in copies:
        copy.wait()


def total_over_depth(n, x):
    vmem = pl.BlockSpec(memory_space=pltpu.VMEM)
    return pl.pallas_call(
        functools.partial(total_kernel, n),
        out_shape=jax.ShapeDtypeStruct(x.shape, F32),
        in_specs=[vmem],
        out_specs=vmem,
        scratch_shapes=[pltpu.VMEM(x.shape, F32), pltpu.VMEM(x.shape[1:], F32)]
        + [pltpu.SemaphoreType.DMA((n,))] * 4,
        compiler_params=pltpu.CompilerParams(collective_id=2, has_side_effects=True),
        name="total_over_depth",
    )(x)


def block_weights(w_first, w_second, planes):
    halves = planes // PACK
    eye = jnp.eye(PACK, dtype=BF)
    w1 = jnp.kron(eye, w_first)
    rad = jnp.kron(eye, w_second[:-1])
    spot = jnp.eye(planes, dtype=BF).reshape(planes, halves, PACK)
    dens = jnp.einsum("phk,j->hpkj", spot, w_second[-1]).reshape(halves, planes, -1)
    rad = jnp.broadcast_to(rad, (halves,) + rad.shape)
    half = jnp.asarray(0.5, BF)
    w2 = jnp.concatenate([rad * half, dens], 1)
    w2t = jnp.concatenate([rad, dens], 1).swapaxes(1, 2) * half
    return w1 * half, w2, w1.T, w2t


def shards(voxels, offsets, w_first, w_second, cotangent):
    planes, feats, rays = voxels.shape
    hid = w_first.shape[0]
    chans, chunk = cotangent.shape
    n = lax.axis_size("depth")
    halves = planes // PACK
    dscale = 3.0 / (planes * n)
    block = min(512, chunk)
    per = chunk // block
    steps = rays // block
    my_off = lax.dynamic_slice_in_dim(offsets, lax.axis_index("depth") * planes, planes)
    w1, w2, w1t, w2t = block_weights(w_first, w_second, planes)
    cot = lax.all_gather(cotangent.astype(BF), "depth")

    smem = pl.BlockSpec(memory_space=pltpu.SMEM)
    vmem = pl.BlockSpec(memory_space=pltpu.VMEM)

    def ray_spec(rows):
        return pl.BlockSpec((1, rows, block), lambda i: (i // per, 0, i % per))

    params = pltpu.CompilerParams(vmem_limit_bytes=60 * 2**20)
    colour, last = pl.pallas_call(
        functools.partial(forward_kernel, dscale),
        grid=(steps,),
        out_shape=(
            jax.ShapeDtypeStruct((n, chans, chunk), F32),
            jax.ShapeDtypeStruct((n, 1, chunk), F32),
        ),
        in_specs=[smem] + [vmem] * 3,
        out_specs=(ray_spec(chans), ray_spec(1)),
        scratch_shapes=[
            pltpu.VMEM((planes * feats, block), BF),
            pltpu.VMEM((planes * chans, block), F32),
        ],
        compiler_params=params,
        cost_estimate=pl.CostEstimate(
            flops=8 * 10**9, bytes_accessed=12 * 2**20, transcendentals=10**7
        ),
        name="forward",
    )(my_off, voxels, w1, w2)
    state = exchange_state(n, last, colour, cot)
    share = (state[:, 0:1, :] * colour).astype(BF)
    image = lax.psum_scatter(share, "depth", scatter_dimension=0).astype(F32)
    ones = jnp.kron(jnp.eye(planes, dtype=BF), jnp.ones((1, chans), BF))
    rows = PACK * chans + planes
    gvox, acc1, acc2 = pl.pallas_call(
        functools.partial(backward_kernel, dscale),
        grid=(steps,),
        out_shape=(
            jax.ShapeDtypeStruct(voxels.shape, BF),
            jax.ShapeDtypeStruct((PACK * hid, PACK * feats), F32),
            jax.ShapeDtypeStruct((halves, rows, PACK * hid), F32),
        ),
        in_specs=[smem] + [vmem] * 6 + [ray_spec(chans), ray_spec(2)],
        out_specs=(vmem, vmem, vmem),
        scratch_shapes=[
            pltpu.VMEM((planes * feats, block), BF),
            pltpu.VMEM((planes * hid, block), F32),
            pltpu.VMEM((8, 128), F32),
            pltpu.VMEM((planes * hid, block), BF),
            pltpu.VMEM((planes * chans, block), F32),
            pltpu.VMEM((halves, rows, block), BF),
            pltpu.VMEM((planes * chans, block), BF),
        ],
        compiler_params=params,
        cost_estimate=pl.CostEstimate(
            flops=60 * 10**9, bytes_accessed=24 * 2**20, transcendentals=10**7
        ),
        name="backward",
    )(my_off, voxels, w1, w2, w1t, w2t, ones, cot, state)
    g1 = sum(
        acc1[k * hid : (k + 1) * hid, k * feats : (k + 1) * feats] for k in range(PACK)
    )
    g2 = jnp.zeros((chans, hid), F32)
    gd = jnp.zeros((1, hid), F32)
    for h in range(halves):
        for k in range(PACK):
            cols = slice(k * hid, (k + 1) * hid)
            row = PACK * chans + h * PACK + k
            g2 = g2 + acc2[h, k * chans : (k + 1) * chans, cols]
            gd = gd + acc2[h, row : row + 1, cols]
    flat = jnp.concatenate([g1.reshape(-1), g2.reshape(-1), gd.reshape(-1)])
    piece = -(-flat.size // (n * 128)) * 128
    padded = jnp.pad(flat, (0, n * piece - flat.size)).reshape(n, 1, piece)
    summed = total_over_depth(n, padded).reshape(-1)
    cut = g1.size
    grad_first = summed[:cut].reshape(g1.shape)
    grad_second = summed[cut : flat.size].reshape(chans + 1, hid)
    return image, gvox, grad_first, grad_second


def solution(mesh):
    placed = (
        P(("groups", "depth"), None, None),
        P("groups"),
        P(),
        P(),
        P(None, ("groups", "depth")),
    )
    return jax.shard_map(
        shards,
        mesh=mesh,
        in_specs=placed,
        out_specs=(
            P(None, ("groups", "depth")),
            P(("groups", "depth"), None, None),
            P("groups", None),
            P("groups", None),
        ),
        check_vma=False,
    )
```

time: 512 us -> 162 us (0.32)
  waiting for transfers between devices: 155 us -> 4.23 us
  Pallas kernels: 0 us -> 124 us
  matrix products: 116 us -> 0 us
  local copies, waits for them, and re-layouts: 79.1 us -> 7.37 us
  other arithmetic: 72.1 us -> 11 us
  blocking collectives: 60.3 us -> 0 us
  loops' own time: 12 us -> 0 us
    pallas_call x0 -> x4, Pallas kernels: none -> 124 us  [the longest x1 65.6 us: shards(): pl.pallas_call(functools.partial(backward_kernel, dscale), grid=(steps,),...]
    dot_general x56 -> x0, matrix products: 116 us -> none  [the longest x8 37.7 us: decode_plane(): preact = jnp.dot(w_first, plane, preferred_element_type=jnp.float32)]
    psum x1 -> x0, waiting for transfers between devices: 85.3 us -> none  [shards(): ray_total = lax.psum(enter * running[-1], 'depth')]
    all_gather x3 -> x1, waiting for transfers between devices: 69.4 us -> 4.2 us  [shards(): cot = lax.all_gather(cotangent.astype(BF), 'depth')]
    psum x1 -> x0, blocking collectives: 60.3 us -> none  [shards(): grad_first, grad_second = lax.psum((grads[0], grads[1]), 'depth')]
    while x81 -> x0, local copies, waits for them, and re-layouts: 32.7 us -> none
    dynamic_slice x33 -> x1, local copies, waits for them, and re-layouts: 28.3 us -> 1.24 us  [shards(): lax.dynamic_slice_in_dim(offsets, lax.axis_index('depth') * planes, planes)]
    dynamic_update_slice x8 -> x0, other arithmetic: 18.2 us -> none  [shards(): slabs = lax.map(forward_plane, (voxels, my_offsets))]
  transfers between devices with their start and end apart: 5 -> 2, of which waited for: 3 -> 1; matrix products, arithmetic and copies ran while one was open for 42% -> 8% of each run, Pallas kernels for 0% -> 67%
where the time goes in v1:
time: 162 us; the launch traced here: 161 us
  Pallas kernels  124 us (77%)
  between operations  14.2 us (9%)
  other arithmetic  11 us (7%)
  local copies, waits for them, and re-layouts  7.37 us (5%)
  waiting for transfers between devices  4.23 us (3%)
    pallas_call x1, Pallas kernels, shards(): pl.pallas_call(functools.partial(backward_kernel, dscale), grid=(steps,),...  65.6 us
    pallas_call x1, Pallas kernels, shards(): pl.pallas_call(functools.partial(forward_kernel, dscale), grid=(steps,),...  30.3 us
    pallas_call x1, Pallas kernels, exchange_state(): pl.pallas_call(functools.partial(state_kernel, n), out_shape=jax.ShapeDty...  15.6 us
    pallas_call x1, Pallas kernels, total_over_depth(): pl.pallas_call(functools.partial(total_kernel, n), out_shape=jax.ShapeDty...  12.7 us
    all_gather x1, waiting for transfers between devices, shards(): cot = lax.all_gather(cotangent.astype(BF), 'depth')  4.2 us
  transfers between devices with their start and end apart: 2, of which 1 were waited for; matrix products, arithmetic and copies ran while one was open for 8% of the time, Pallas kernels for 67%

profile of v1, /device:TPU:0, one launch (start us, length us, event | category | flops | bytes accessed | tf_op | source)
XLA Modules:
  0.0 161.0 jit_solution(6127219143772657434)
XLA Ops:
  7.2 0.0 all-gather.3.cloned.1.call-start
  7.2 1.5 convert_element_type.32
  8.7 0.0 all-gather.3.cloned.1.call-update
  8.8 0.0 reduce-scatter.2.cloned.1.call-start
  8.8 0.7 slice_bitcast_fusion
  9.5 0.7 slice.81
  10.2 0.1 copy.15
  10.3 0.1 iota.67
  10.4 0.1 fusion.1
  10.5 0.1 broadcast_multiply_fusion.1
  10.6 0.1 mul.122
  10.7 0.7 mul.123.ones_ref
  11.4 0.1 mul.113
  11.5 0.1 copy.18
  11.7 0.1 broadcast_multiply_fusion
  11.7 0.1 copy.16
  11.8 0.8 broadcast_multiply_fusion.2
  12.7 0.1 mul.107
  12.8 0.0 copy-start.1
  12.8 0.7 copy.17.w1_ref
  13.6 1.2 dynamic_slice.3.off_ref
  14.8 0.7 pad_maximum_fusion.w2_ref
  15.5 0.8 fusion.w2t_ref
  16.3 30.3 %forward.1 = (f32[16,32,1024]{2,1,0:T(8,128)}, f32[16,1,1024]{2,1,0:T(1,128)}) custom-call(s32[8]{0:T(128)} %dynamic_slice.3.off_ref, bf16[8,32,16384]{2,1,0:T(8,128)(2,1)} %vox_ref.3, bf16[256,128]{1,0:T(8,128)(2,1)} %copy.17.w1_ref, bf16[2,136,256]{2,1,0:T(8,128)(2,1)} %pad_maximum_fusion.w2_ref), custom_call_target="tpu_custom_call" | custom-call | flops 8000000000 | bytes 12582912 | tf_op jit(solution)/shard_map/forward/pallas_call | solution.py:308
  46.6 0.0 copy-done.1
  46.6 0.0 copy-start
  46.6 4.2 %all-gather.3.cloned.1.call-done = bf16[512,1024]{1,0:T(8,128)(2,1)} async-done(((bf16[32,1024]{1,0:T(8,128)(2,1)}), bf16[512,1024]{1,0:T(8,128)(2,1)}) %all-gather.3.cloned.1.call-update) | async-done | bytes 1048592 | tf_op jit(solution)/shard_map/all_gather | solution.py:299
  50.8 15.6 %exchange_state.1.state_ref = f32[16,2,1024]{2,1,0:T(2,128)} custom-call(f32[16,1,1024]{2,1,0:T(1,128)} %get-tuple-element.9.last_ref, f32[16,32,1024]{2,1,0:T(8,128)} %get-tuple-element.10.col_ref, bf16[16,32,1024]{2,1,0:T(8,128)(2,1)} %bitcast.23), custom_call_target="tpu_custom_call" | custom-call | tf_op jit(solution)/shard_map/exchange_state/pallas_call | solution.py:234
  66.4 1.0 slice.83
  67.4 0.0 copy-done
  67.4 1.3 multiply_convert_fusion
  68.6 0.0 reduce-scatter.2.cloned.1.call-update
  68.7 65.6 %backward.1 = (bf16[8,32,16384]{2,1,0:T(8,128)(2,1)}, f32[256,128]{1,0:T(8,128)}, f32[2,136,256]{2,1,0:T(8,128)}) custom-call(s32[8]{0:T(128)} %dynamic_slice.3.off_ref, bf16[8,32,16384]{2,1,0:T(8,128)(2,1)} %vox_ref.3, bf16[256,128]{1,0:T(8,128)(2,1)} %copy.17.w1_ref, bf16[2,136,256]{2,1,0:T(8,128)(2,1)} %pad_maximum_fusion.w2_ref, ...), custom_call_target="tpu_custom_call" | custom-call | flops 60000002048 | bytes 25165824 | tf_op jit(solution)/shard_map/backward/pallas_call | solution.py:332
  134.3 0.9 add_add_fusion
  135.2 0.1 reshape.166
  135.3 0.9 slice_add_fusion
  136.2 0.1 reshape.158
  136.3 0.9 add_bitcast_fusion
  137.1 0.6 select_maximum_fusion
  137.8 12.7 %total_over_depth.1 = f32[16,1,384]{2,1,0:T(1,128)} custom-call(f32[16,1,384]{2,1,0:T(1,128)} %bitcast.27), custom_call_target="tpu_custom_call" | custom-call | tf_op jit(solution)/shard_map/total_over_depth/pallas_call | solution.py:261
  150.4 0.8 reduce
  151.2 0.1 slice.106
  151.3 0.1 slice.104
  151.4 0.6 slice.109
  152.0 0.7 copy.20
  152.7 0.0 reduce-scatter.2.cloned.1.call-done
  152.7 1.5 bitcast_convert_fusion
  (9 shorter events, 0.1 us)
Async XLA Ops:
  7.2 43.7 %all-gather.3.cloned.1.call-start = ((), (), s32[]{:S(2)}) async-start(), calls=%async_computation.2 | async-start | bytes 1114112 | tf_op jit(solution)/shard_map/all_gather | solution.py:299
  8.8 143.9 %reduce-scatter.2.cloned.1.call-start = ((), (), s32[]{:S(2)}) async-start(), calls=%async_computation.1 | async-start | bytes 1114112 | tf_op jit(solution)/shard_map/reduce_scatter | solution.py:329
  12.8 33.8 %copy-start.1 = (bf16[256,128]{0,1:T(8,128)(2,1)}, bf16[256,128]{0,1:T(8,128)(2,1)S(1)}, u32[]{:S(2)}) copy-start(bf16[256,128]{0,1:T(8,128)(2,1)S(1)} %mul.107) | copy-start | bytes 196612
  46.6 20.7 %copy-start = (f32[16,32,1024]{2,1,0:T(8,128)S(1)}, f32[16,32,1024]{2,1,0:T(8,128)}, u32[]{:S(2)}) copy-start(f32[16,32,1024]{2,1,0:T(8,128)} %get-tuple-element.10.col_ref) | copy-start | bytes 6291460
Sparse Core Ops, SparseCore 0:
  10.1 40.6 all-gather.2
  68.8 56.9 reduce-scatter.1

commit v2 on v1

v2 whole, which is shorter than its diff:
```python
import functools

import jax
import jax.numpy as jnp
from jax import lax
from jax.experimental import pallas as pl
from jax.experimental.pallas import tpu as pltpu
from jax.sharding import PartitionSpec as P

TILE = 128
PACK = 4
BLOCK = 1024
FSUB = 1024
BSUB = 1024
BF = jnp.bfloat16
F32 = jnp.float32
NT = (((1,), (1,)), ((), ()))


def dot(a, b):
    return jnp.dot(a, b, preferred_element_type=F32)


def running_sum(x):
    rows = x.shape[0]
    row = lax.broadcasted_iota(jnp.int32, x.shape, 0)
    s = 1
    while s < rows:
        x = x + jnp.where(row >= s, pltpu.roll(x, s, 0), 0.0)
        s *= 2
    return x


def wrap(t, total):
    if total & (total - 1) == 0:
        return t & (total - 1)
    return lax.rem(t, total)


def first_tile(off_ref, planes, p):
    return off_ref[lax.axis_index("depth") * planes + p]


def tile_at(base, j, rays):
    return pl.ds(pl.multiple_of(wrap(base + j, rays // TILE) * TILE, TILE), TILE)


def gather_tiles(off_ref, vox_ref, x_ref, step):
    planes, feats, rays = vox_ref.shape
    tiles = x_ref.shape[1] // TILE
    for p in range(planes):
        base = step * tiles + first_tile(off_ref, planes, p)
        for j in range(tiles):
            x_ref[pl.ds(p * feats, feats), pl.ds(j * TILE, TILE)] = vox_ref[
                p, :, tile_at(base, j, rays)
            ]


def absorb(dens):
    upto = running_sum(dens)
    passing = jnp.exp(-dens)
    before = jnp.exp(dens - upto)
    return upto, passing, before


def softplus(x):
    return jnp.maximum(x, 0.0) + jnp.log1p(jnp.exp(-jnp.abs(x)))


def picks(shape, period, dim):
    other = lax.broadcasted_iota(jnp.int32, shape, 1 - dim)
    return (lax.rem(lax.broadcasted_iota(jnp.int32, shape, dim), period) == other).astype(BF)


def diagonal(shape, rows, cols):
    r = lax.broadcasted_iota(jnp.int32, shape, 0) // rows
    return r == lax.broadcasted_iota(jnp.int32, shape, 1) // cols


def repeat_blocks(w):
    rows, cols = w.shape
    tall = dot(picks((PACK * rows, rows), rows, 0), w).astype(BF)
    full = dot(tall, picks((cols, PACK * cols), cols, 1))
    return jnp.where(diagonal(full.shape, rows, cols), full, 0.0)


def prepare(first_ref, second_ref, w1_ref, w1t_ref, w2_ref, w2t_ref):
    planes = PACK * w2_ref.shape[0]
    chans, hid = second_ref.shape[0] - 1, second_ref.shape[1]
    w1 = repeat_blocks(first_ref[...])
    w1_ref[...] = (0.5 * w1).astype(BF)
    w1t_ref[...] = w1.T.astype(BF)
    rad = repeat_blocks(second_ref[0:chans, :])
    dens = dot(second_ref[chans : chans + 1, :], picks((hid, PACK * hid), hid, 1))
    dens = jnp.broadcast_to(dens, (planes, PACK * hid))
    block = lax.broadcasted_iota(jnp.int32, dens.shape, 1) // hid
    plane = lax.broadcasted_iota(jnp.int32, dens.shape, 0)
    for h in range(planes // PACK):
        mine = jnp.where(plane == block + h * PACK, dens, 0.0)
        w2_ref[h] = jnp.concatenate([0.5 * rad, mine], 0).astype(BF)
        w2t_ref[h] = (0.5 * jnp.concatenate([rad, mine], 0)).T.astype(BF)


def forward_kernel(
    dscale,
    sub,
    off_ref,
    vox_ref,
    first_ref,
    second_ref,
    col_ref,
    last_ref,
    w1_ref,
    w1t_ref,
    w2_ref,
    w2t_ref,
    x_ref,
    rad_ref,
):
    step = pl.program_id(0)

    @pl.when(step == 0)
    def _():
        prepare(first_ref, second_ref, w1_ref, w1t_ref, w2_ref, w2t_ref)

    gather_tiles(off_ref, vox_ref, x_ref, step)
    halves, rows = w2_ref.shape[0], w2_ref.shape[1]
    planes = vox_ref.shape[0]
    wide = rows - planes
    kin = w1_ref.shape[1]
    chans = col_ref.shape[1]
    for c in range(x_ref.shape[1] // sub):
        here = pl.ds(c * sub, sub)
        raw_d = None
        for h in range(halves):
            half = dot(w1_ref[...], x_ref[pl.ds(h * kin, kin), here])
            hidden = (half + half * jnp.tanh(half)).astype(BF)
            raw = dot(w2_ref[h], hidden)
            rad_ref[pl.ds(h * wide, wide), here] = jnp.tanh(raw[:wide])
            d = raw[wide:]
            raw_d = d if raw_d is None else raw_d + d
        dens = softplus(raw_d) * dscale
        upto, passing, before = absorb(dens)
        weight = 0.5 * before * (1.0 - passing)
        colour = jnp.sum(weight, axis=0, keepdims=True)
        for p in range(planes):
            colour = colour + weight[p : p + 1] * rad_ref[pl.ds(p * chans, chans), here]
        col_ref[0, :, here] = colour
        last_ref[0, :, here] = jnp.exp(-upto[planes - 1 : planes])


def backward_kernel(
    dscale,
    sub,
    off_ref,
    vox_ref,
    w1_ref,
    w1t_ref,
    w2_ref,
    w2t_ref,
    cot_ref,
    state_ref,
    gvox_ref,
    acc1_ref,
    acc2_ref,
    x_ref,
    slope_ref,
    hid_ref,
    s_ref,
    graw_ref,
    gpre_ref,
):
    step = pl.program_id(0)

    @pl.when(step == 0)
    def _():
        acc1_ref[...] = jnp.zeros_like(acc1_ref)
        acc2_ref[...] = jnp.zeros_like(acc2_ref)

    gather_tiles(off_ref, vox_ref, x_ref, step)
    halves, rows = w2_ref.shape[0], w2_ref.shape[1]
    planes, feats, rays = vox_ref.shape
    wide = rows - planes
    kin = w1_ref.shape[1]
    kmid = w1_ref.shape[0]
    chans = cot_ref.shape[1]
    width = x_ref.shape[1]
    ones = diagonal((planes, planes * chans), 1, chans).astype(BF)
    for c in range(width // sub):
        here = pl.ds(c * sub, sub)
        cot = cot_ref[0, :, here].astype(F32)
        raw_d = None
        score = 0.5 * jnp.sum(cot, axis=0, keepdims=True)
        for h in range(halves):
            half = dot(w1_ref[...], x_ref[pl.ds(h * kin, kin), here])
            t = jnp.tanh(half)
            up = 1.0 + t
            hidden = half * up
            slope_ref[pl.ds(h * kmid, kmid), here] = up + hidden * (1.0 - t)
            hidden = hidden.astype(BF)
            hid_ref[pl.ds(h * kmid, kmid), here] = hidden
            raw = dot(w2_ref[h], hidden)
            s = jnp.tanh(raw[:wide])
            s_ref[pl.ds(h * wide, wide), here] = s
            prod = jnp.concatenate(
                [(cot * s[k * chans : (k + 1) * chans]).astype(BF) for k in range(PACK)], 0
            )
            score = score + 0.5 * dot(ones[:, h * wide : (h + 1) * wide], prod)
            d = raw[wide:]
            raw_d = d if raw_d is None else raw_d + d
        dens = softplus(raw_d) * dscale
        upto, passing, before = absorb(dens)
        enter = state_ref[0, 0:1, here]
        rest = state_ref[0, 1:2, here]
        before = enter * before
        weight = before * (1.0 - passing)
        running = running_sum(weight * score)
        grad_d = before * passing * score - (rest - running)
        grad_d = (grad_d * (dscale * (0.5 * jnp.tanh(0.5 * raw_d) + 0.5))).astype(BF)
        weight = 0.25 * weight
        for h in range(halves):
            for k in range(PACK):
                p = h * PACK + k
                s = s_ref[pl.ds(p * chans, chans), here]
                graw_ref[h, pl.ds(k * chans, chans), here] = (
                    (weight[p : p + 1] * cot) * (1.0 - s * s)
                ).astype(BF)
            graw_ref[h, pl.ds(wide, planes), here] = grad_d
            ghid = dot(w2t_ref[h], graw_ref[h, :, here])
            gpre = (ghid * slope_ref[pl.ds(h * kmid, kmid), here]).astype(BF)
            gpre_ref[pl.ds(h * kmid, kmid), here] = gpre
            gx = dot(w1t_ref[...], gpre).astype(BF)
            for k in range(PACK):
                p = h * PACK + k
                base = (step * width + c * sub) // TILE + first_tile(off_ref, planes, p)
                for j in range(sub // TILE):
                    gvox_ref[p, :, tile_at(base, j, rays)] = gx[
                        k * feats : (k + 1) * feats, j * TILE : (j + 1) * TILE
                    ]
    for h in range(halves):
        gpre = gpre_ref[pl.ds(h * kmid, kmid), :]
        x = x_ref[pl.ds(h * kin, kin), :]
        hidden = hid_ref[pl.ds(h * kmid, kmid), :]
        acc1_ref[...] += lax.dot_general(gpre, x, NT, preferred_element_type=F32)
        acc2_ref[h] += lax.dot_general(graw_ref[h], hidden, NT, preferred_element_type=F32)


def greet(n, me):
    barrier = pltpu.get_barrier_semaphore()
    for s in range(1, n):
        pl.semaphore_signal(
            barrier,
            inc=1,
            device_id={"depth": lax.rem(me + s, n)},
            device_id_type=pl.DeviceIdType.MESH,
        )
    pl.semaphore_wait(barrier, n - 1)


def swap(n, me, source, target, send_sem, recv_sem):
    copies = []
    for s in range(1, n):
        to = lax.rem(me + s, n)
        copies.append(
            pltpu.make_async_remote_copy(
                src_ref=source(to),
                dst_ref=target.at[me],
                send_sem=send_sem.at[s],
                recv_sem=recv_sem.at[s],
                device_id={"depth": to},
                device_id_type=pl.DeviceIdType.MESH,
            )
        )
    for copy in copies:
        copy.start()
    return copies


def state_kernel(n, last_ref, col_ref, cot_ref, out_ref, mine, got, back, s1, r1, s2, r2):
    me = lax.axis_index("depth")
    greet(n, me)

    def fill(d, carry):
        mine[d, 0:1, :] = last_ref[d]
        mine[d, 1:2, :] = jnp.sum(col_ref[d] * cot_ref[d].astype(F32), axis=0, keepdims=True)
        return carry

    lax.fori_loop(0, n, fill, 0)
    copies = swap(n, me, lambda to: mine.at[to], got, s1, r1)
    got[me] = mine[me]
    for copy in copies:
        copy.wait()
    enter = jnp.ones_like(got[0, 0:1, :])
    prior = jnp.zeros_like(enter)
    for d in range(n):
        back[d, 0:1, :] = enter
        back[d, 1:2, :] = prior
        prior = prior + enter * got[d, 1:2, :]
        enter = enter * got[d, 0:1, :]
    for d in range(n):
        back[d, 1:2, :] = prior - back[d, 1:2, :]
    copies = swap(n, me, lambda to: back.at[to], out_ref, s2, r2)
    out_ref[me] = back[me]
    for copy in copies:
        copy.wait()


def exchange_state(n, last, colour, cot):
    chunk = last.shape[2]
    shape = (n, 2, chunk)
    vmem = pl.BlockSpec(memory_space=pltpu.VMEM)
    return pl.pallas_call(
        functools.partial(state_kernel, n),
        out_shape=jax.ShapeDtypeStruct(shape, F32),
        in_specs=[vmem] * 3,
        out_specs=vmem,
        scratch_shapes=[pltpu.VMEM(shape, F32)] * 3 + [pltpu.SemaphoreType.DMA((n,))] * 4,
        compiler_params=pltpu.CompilerParams(collective_id=1, has_side_effects=True),
        name="exchange_state",
    )(last, colour, cot)


def total_kernel(n, a1_ref, a2_ref, g1_ref, g2_ref, give, got, mine, full, s1, r1, s2, r2):
    me = lax.axis_index("depth")
    greet(n, me)
    hid, feats = g1_ref.shape
    chans = g2_ref.shape[0] - 1
    halves, rows = a2_ref.shape[0], a2_ref.shape[1]
    part = give.shape[1]

    def aligned(ref_rows, k, size):
        at = k * size
        lane = at % TILE
        piece = ref_rows[:, at - lane : at - lane + TILE]
        return pltpu.roll(piece, TILE - lane, 1) if lane else piece

    g1 = g2 = gd = None
    for k in range(PACK):
        one = aligned(a1_ref[pl.ds(k * hid, hid), :], k, feats)
        g1 = one if g1 is None else g1 + one
    for h in range(halves):
        tail = a2_ref[h, pl.ds(PACK * chans, rows - PACK * chans), :]
        row = lax.broadcasted_iota(jnp.int32, (tail.shape[0], TILE), 0)
        for k in range(PACK):
            two = aligned(a2_ref[h, pl.ds(k * chans, chans), :], k, hid)
            g2 = two if g2 is None else g2 + two
            dens = jnp.where(row == h * PACK + k, aligned(tail, k, hid), 0.0)
            dens = jnp.sum(dens, axis=0, keepdims=True)
            gd = dens if gd is None else gd + dens
    lanes = lax.broadcasted_iota(jnp.int32, (hid, TILE), 1)
    rest = hid - chans - 1
    low = jnp.concatenate([g2, gd, jnp.zeros((rest, TILE), F32)], 0)
    both = jnp.where(lanes < hid, low, pltpu.roll(g1, hid, 1))
    for d in range(n):
        give[d] = both[d * part : (d + 1) * part]
    copies = swap(n, me, lambda to: give.at[to], got, s1, r1)
    got[me] = give[me]
    for copy in copies:
        copy.wait()
    mine[...] = jnp.sum(got[...], axis=0)
    copies = swap(n, me, lambda to: mine, full, s2, r2)
    full[me] = mine[...]
    for copy in copies:
        copy.wait()
    both = jnp.concatenate([full[d] for d in range(n)], 0)
    g2_ref[...] = both[: chans + 1, :hid]
    g1_ref[...] = pltpu.roll(both, TILE - hid, 1)[:, :feats]


def total_over_depth(n, acc1, acc2, first, second):
    vmem = pl.BlockSpec(memory_space=pltpu.VMEM)
    part = (n, first[0] // n, TILE)
    return pl.pallas_call(
        functools.partial(total_kernel, n),
        out_shape=(jax.ShapeDtypeStruct(first, F32), jax.ShapeDtypeStruct(second, F32)),
        in_specs=[vmem] * 2,
        out_specs=(vmem, vmem),
        scratch_shapes=[
            pltpu.VMEM(part, F32),
            pltpu.VMEM(part, F32),
            pltpu.VMEM(part[1:], F32),
            pltpu.VMEM(part, F32),
        ]
        + [pltpu.SemaphoreType.DMA((n,))] * 4,
        compiler_params=pltpu.CompilerParams(collective_id=2, has_side_effects=True),
        name="total_over_depth",
    )(acc1, acc2)


def shards(voxels, offsets, w_first, w_second, cotangent):
    planes, feats, rays = voxels.shape
    hid = w_first.shape[0]
    chans, chunk = cotangent.shape
    n = lax.axis_size("depth")
    halves = planes // PACK
    dscale = 3.0 / (planes * n)
    block = min(BLOCK, chunk)
    per = chunk // block
    steps = rays // block
    cot = lax.all_gather(cotangent.astype(BF), "depth")

    smem = pl.BlockSpec(memory_space=pltpu.SMEM)
    vmem = pl.BlockSpec(memory_space=pltpu.VMEM)

    def ray_spec(rows):
        return pl.BlockSpec((1, rows, block), lambda i: (i // per, 0, i % per))

    params = pltpu.CompilerParams(vmem_limit_bytes=60 * 2**20)
    rows = PACK * chans + planes
    weights = (
        jax.ShapeDtypeStruct((PACK * hid, PACK * feats), BF),
        jax.ShapeDtypeStruct((PACK * feats, PACK * hid), BF),
        jax.ShapeDtypeStruct((halves, rows, PACK * hid), BF),
        jax.ShapeDtypeStruct((halves, PACK * hid, rows), BF),
    )
    colour, last, *weights = pl.pallas_call(
        functools.partial(forward_kernel, dscale, min(FSUB, block)),
        grid=(steps,),
        out_shape=(
            jax.ShapeDtypeStruct((n, chans, chunk), F32),
            jax.ShapeDtypeStruct((n, 1, chunk), F32),
        )
        + weights,
        in_specs=[smem] + [vmem] * 3,
        out_specs=(ray_spec(chans), ray_spec(1)) + (vmem,) * 4,
        scratch_shapes=[
            pltpu.VMEM((planes * feats, block), BF),
            pltpu.VMEM((planes * chans, block), F32),
        ],
        compiler_params=params,
        cost_estimate=pl.CostEstimate(
            flops=8 * 10**9, bytes_accessed=12 * 2**20, transcendentals=10**7
        ),
        name="forward",
    )(offsets, voxels, w_first, w_second)
    state = exchange_state(n, last, colour, cot)
    share = (state[:, 0:1, :] * colour).astype(BF)
    image = lax.psum_scatter(share, "depth", scatter_dimension=0).astype(F32)
    gvox, acc1, acc2 = pl.pallas_call(
        functools.partial(backward_kernel, dscale, min(BSUB, block)),
        grid=(steps,),
        out_shape=(
            jax.ShapeDtypeStruct(voxels.shape, BF),
            jax.ShapeDtypeStruct((PACK * hid, PACK * feats), F32),
            jax.ShapeDtypeStruct((halves, rows, PACK * hid), F32),
        ),
        in_specs=[smem] + [vmem] * 5 + [ray_spec(chans), ray_spec(2)],
        out_specs=(vmem, vmem, vmem),
        scratch_shapes=[
            pltpu.VMEM((planes * feats, block), BF),
            pltpu.VMEM((planes * hid, block), F32),
            pltpu.VMEM((planes * hid, block), BF),
            pltpu.VMEM((planes * chans, block), F32),
            pltpu.VMEM((halves, rows, block), BF),
            pltpu.VMEM((planes * hid, block), BF),
        ],
        compiler_params=params,
        cost_estimate=pl.CostEstimate(
            flops=60 * 10**9, bytes_accessed=24 * 2**20, transcendentals=10**7
        ),
        name="backward",
    )(offsets, voxels, *weights, cot, state)
    grad_first, grad_second = total_over_depth(n, acc1, acc2, w_first.shape, w_second.shape)
    return image, gvox, grad_first, grad_second


def solution(mesh):
    placed = (
        P(("groups", "depth"), None, None),
        P("groups"),
        P(),
        P(),
        P(None, ("groups", "depth")),
    )
    return jax.shard_map(
        shards,
        mesh=mesh,
        in_specs=placed,
        out_specs=(
            P(None, ("groups", "depth")),
            P(("groups", "depth"), None, None),
            P("groups", None),
            P("groups", None),
        ),
        check_vma=False,
    )
```

time: 162 us -> 142 us (0.88)
  Pallas kernels: 124 us -> 99.1 us
  waiting for transfers between devices: 4.23 us -> 19.1 us
  other arithmetic: 11 us -> 4.3 us
  local copies, waits for them, and re-layouts: 7.37 us -> 5.13 us
    pallas_call x3, Pallas kernels: 109 us -> 83.6 us  [the longest x1 48.7 us: shards(): pl.pallas_call(functools.partial(backward_kernel, dscale, min(BSUB, block...]
    all_gather x1, waiting for transfers between devices: 4.2 us -> 19.1 us  [shards(): cot = lax.all_gather(cotangent.astype(BF), 'depth')]
    unnamed x6, local copies, waits for them, and re-layouts: 0.7 us -> 4.18 us
    add x3 -> x0, other arithmetic: 2.69 us -> none  [the longest x1 0.92 us: shards(): g2 = g2 + acc2[h, k * chans:(k + 1) * chans, cols]]
    mul x6 -> x0, local copies, waits for them, and re-layouts: 1.9 us -> none  [the longest x2 0.76 us: shards(): ones = jnp.kron(jnp.eye(planes, dtype=BF), jnp.ones((1, chans), BF))]
    mul x5 -> x0, other arithmetic: 1.72 us -> none  [the longest x1 0.83 us: block_weights(): w1 = jnp.kron(eye, w_first)]
  transfers between devices with their start and end apart: 2 -> 2, of which waited for: 1 -> 1; matrix products, arithmetic and copies ran while one was open for 8% -> 2% of each run, Pallas kernels for 67% -> 59%
where the time goes in v2:
time: 142 us
  Pallas kernels  99.1 us (70%)
  waiting for transfers between devices  19.1 us (13%)
  between operations  14.1 us (10%)
  local copies, waits for them, and re-layouts  5.13 us (4%)
  other arithmetic  4.3 us (3%)
    pallas_call x1, Pallas kernels, shards(): pl.pallas_call(functools.partial(backward_kernel, dscale, min(BSUB, block...  48.7 us
    pallas_call x1, Pallas kernels, shards(): pl.pallas_call(functools.partial(forward_kernel, dscale, min(FSUB, block)...  21.5 us
    all_gather x1, waiting for transfers between devices, shards(): cot = lax.all_gather(cotangent.astype(BF), 'depth')  19.1 us
    pallas_call x1, Pallas kernels, exchange_state(): pl.pallas_call(functools.partial(state_kernel, n), out_shape=jax.ShapeDty...  15.4 us
    pallas_call x1, Pallas kernels, total_over_depth(): pl.pallas_call(functools.partial(total_kernel, n), out_shape=(jax.ShapeDt...  13.4 us
    unnamed x6, local copies, waits for them, and re-layouts  4.18 us
  transfers between devices with their start and end apart: 2, of which 1 were waited for; matrix products, arithmetic and copies ran while one was open for 2% of the time, Pallas kernels for 59%

profile of v2, /device:TPU:0, one launch (start us, length us, event | category | flops | bytes accessed | tf_op | source)
XLA Modules:
  0.0 141.8 jit_solution(14210683310734121945)
XLA Ops:
  7.2 0.0 all-gather.3.cloned.1.call-start
  7.2 1.5 %convert_element_type.12 = bf16[32,1024]{1,0:T(8,128)(2,1)} convert(f32[32,1024]{1,0:T(8,128)} %param.9) | non-fusion elementwise | flops 32768 | bytes 196608 | tf_op jit(solution)/shard_map/convert_element_type | solution.py:400
  8.7 0.0 all-gather.3.cloned.1.call-update
  8.8 0.0 reduce-scatter.2.cloned.1.call-start
  8.8 1.4 copy.9.first_ref
  10.2 21.5 %forward.1 = (f32[16,32,1024]{2,1,0:T(8,128)}, f32[16,1,1024]{2,1,0:T(1,128)}, bf16[256,128]{1,0:T(8,128)(2,1)}, bf16[128,256]{1,0:T(8,128)(2,1)}, bf16[2,136,25...) custom-call(s32[128]{0:T(128)} %off_ref.3, bf16[8,32,16384]{2,1,0:T(8,128)(2,1)} %vox_ref.3, bf16[64,32]{1,0:T(8,128)(2,1)} %copy.9.first_ref, ...), custom_call_target="tpu_custom_call" | custom-call | flops 8000000000 | bytes 12582912 | tf_op jit(solution)/shard_map/forward/pallas_call | solution.py:416
  31.7 0.0 copy-start
  31.7 19.1 %all-gather.3.cloned.1.call-done = bf16[512,1024]{1,0:T(8,128)(2,1)} async-done(((bf16[32,1024]{1,0:T(8,128)(2,1)}), bf16[512,1024]{1,0:T(8,128)(2,1)}) %all-gather.3.cloned.1.call-update) | async-done | bytes 1048592 | tf_op jit(solution)/shard_map/all_gather | solution.py:400
  50.8 15.4 %exchange_state.1.state_ref = f32[16,2,1024]{2,1,0:T(2,128)} custom-call(f32[16,1,1024]{2,1,0:T(1,128)} %get-tuple-element.15.last_ref, f32[16,32,1024]{2,1,0:T(8,128)} %get-tuple-element.16.col_ref, bf16[16,32,1024]{2,1,0:T(8,128)(2,1)} %bitcast.7), custom_call_target="tpu_custom_call" | custom-call | tf_op jit(solution)/shard_map/exchange_state/pallas_call | solution.py:312
  66.2 1.0 slice.3
  67.2 0.0 copy-done
  67.2 1.3 multiply_convert_fusion
  68.5 0.0 reduce-scatter.2.cloned.1.call-update
  68.5 48.7 %backward.1 = (bf16[8,32,16384]{2,1,0:T(8,128)(2,1)}, f32[256,128]{1,0:T(8,128)}, f32[2,136,256]{2,1,0:T(8,128)}) custom-call(s32[128]{0:T(128)} %off_ref.3, bf16[8,32,16384]{2,1,0:T(8,128)(2,1)} %vox_ref.3, bf16[256,128]{1,0:T(8,128)(2,1)} %get-tuple-element.17.w1_ref, bf16[128,256]{1,0:T(8,128)(2,1)} %get-tuple-element.18.w1t_ref, ...), custom_call_target="tpu_custom_call" | custom-call | flops 60000002048 | bytes 25165824 | tf_op jit(solution)/shard_map/backward/pallas_call | solution.py:439
  117.2 13.4 %total_over_depth.1 = (f32[64,32]{1,0:T(8,128)}, f32[33,64]{1,0:T(8,128)}) custom-call(f32[256,128]{1,0:T(8,128)} %get-tuple-element.22.a1_ref, f32[2,136,256]{2,1,0:T(8,128)} %get-tuple-element.23.a2_ref), custom_call_target="tpu_custom_call" | custom-call | tf_op jit(solution)/shard_map/total_over_depth/pallas_call | solution.py:373
  130.7 1.4 %copy.10 = f32[64,32]{0,1:T(8,128)} copy(f32[64,32]{1,0:T(8,128)} %get-tuple-element.28) | data formatting | bytes 16384
  132.1 0.0 reduce-scatter.2.cloned.1.call-done
  132.1 1.5 %bitcast_convert_fusion = f32[32,1024]{1,0:T(8,128)} fusion(bf16[1,32,1024]{2,1,0:T(8,128)(2,1)} %reduce-scatter.2.cloned.1.call-done), kind=kLoop, calls=%fused_computation.2 | loop fusion | flops 32768 | bytes 196608 | tf_op jit(solution)/shard_map/convert_element_type | solution.py:438
  133.6 1.3 copy.15
  (1 shorter events, 0.0 us)
Async XLA Ops:
  7.2 43.6 %all-gather.3.cloned.1.call-start = ((), (), s32[]{:S(2)}) async-start(), calls=%async_computation.2 | async-start | bytes 1114112 | tf_op jit(solution)/shard_map/all_gather | solution.py:400
  8.8 123.4 %reduce-scatter.2.cloned.1.call-start = ((), (), s32[]{:S(2)}) async-start(), calls=%async_computation.1 | async-start | bytes 1114112 | tf_op jit(solution)/shard_map/reduce_scatter | solution.py:438
  31.7 35.5 %copy-start = (f32[16,32,1024]{2,1,0:T(8,128)S(1)}, f32[16,32,1024]{2,1,0:T(8,128)}, u32[]{:S(2)}) copy-start(f32[16,32,1024]{2,1,0:T(8,128)} %get-tuple-element.16.col_ref) | copy-start | bytes 6291460
Sparse Core Ops, SparseCore 0:
  10.1 40.5 all-gather.2
  68.6 57.0 reduce-scatter.1

commit v3 on v2

--- a/solution.py
+++ b/solution.py
@@ -12,6 +12,7 @@
 BLOCK = 1024
 FSUB = 1024
 BSUB = 1024
+RELAY = 12
 BF = jnp.bfloat16
 F32 = jnp.float32
 NT = (((1,), (1,)), ((), ()))
@@ -45,15 +46,26 @@
     return pl.ds(pl.multiple_of(wrap(base + j, rays // TILE) * TILE, TILE), TILE)
 
 
-def gather_tiles(off_ref, vox_ref, x_ref, step):
-    planes, feats, rays = vox_ref.shape
-    tiles = x_ref.shape[1] // TILE
-    for p in range(planes):
-        base = step * tiles + first_tile(off_ref, planes, p)
-        for j in range(tiles):
-            x_ref[pl.ds(p * feats, feats), pl.ds(j * TILE, TILE)] = vox_ref[
-                p, :, tile_at(base, j, rays)
-            ]
+def shear_kernel(off_ref, vox_ref, x_ref):
+    rays = vox_ref.shape[2]
+    base = first_tile(off_ref, pl.num_programs(0), pl.program_id(0))
+    for j in range(rays // TILE):
+        x_ref[:, pl.ds(j * TILE, TILE)] = vox_ref[0, :, tile_at(base, j, rays)]
+
+
+def shear(offsets, voxels):
+    planes, feats, rays = voxels.shape
+    return pl.pallas_call(
+        shear_kernel,
+        grid=(planes,),
+        out_shape=jax.ShapeDtypeStruct((planes * feats, rays), BF),
+        in_specs=[
+            pl.BlockSpec(memory_space=pltpu.SMEM),
+            pl.BlockSpec((1, feats, rays), lambda p: (p, 0, 0)),
+        ],
+        out_specs=pl.BlockSpec((feats, rays), lambda p: (p, 0)),
+        name="shear",
+    )(offsets, voxels)
 
 
 def absorb(dens):
@@ -104,28 +116,75 @@
 def forward_kernel(
     dscale,
     sub,
-    off_ref,
-    vox_ref,
+    x_ref,
     first_ref,
     second_ref,
+    cot_ref,
     col_ref,
-    last_ref,
+    cots_ref,
+    state_ref,
     w1_ref,
     w1t_ref,
     w2_ref,
     w2t_ref,
-    x_ref,
     rad_ref,
+    cots,
+    mine,
+    got,
+    back,
+    land,
+    sa,
+    ra,
+    sb,
+    rb,
+    s1,
+    r1,
+    s2,
+    r2,
 ):
     step = pl.program_id(0)
+    steps = pl.num_programs(0)
+    n = mine.shape[0]
+    me = lax.axis_index("depth")
+    chip, core = me // 2, lax.rem(me, 2)
+
+    def across_chips(s):
+        return pltpu.make_async_remote_copy(
+            src_ref=cots.at[chip, core],
+            dst_ref=cots.at[chip, core],
+            send_sem=sa.at[s],
+            recv_sem=ra.at[s],
+            device_id={"depth": lax.rem(me + 2 * s, n)},
+            device_id_type=pl.DeviceIdType.MESH,
+        )
+
+    def to_partner():
+        return pltpu.make_async_remote_copy(
+            src_ref=cots.at[:, core],
+            dst_ref=cots.at[:, core],
+            send_sem=sb,
+            recv_sem=rb,
+            device_id={"depth": me + 1 - 2 * core},
+            device_id_type=pl.DeviceIdType.MESH,
+        )
 
     @pl.when(step == 0)
     def _():
+        cots[chip, core] = cot_ref[...].astype(BF)
+        greet(n, me)
+        for s in range(1, n // 2):
+            across_chips(s).start()
         prepare(first_ref, second_ref, w1_ref, w1t_ref, w2_ref, w2t_ref)
 
-    gather_tiles(off_ref, vox_ref, x_ref, step)
+    @pl.when(step == RELAY * steps // 16)
+    def _():
+        for s in range(1, n // 2):
+            across_chips(s).wait()
+        to_partner().start()
+
     halves, rows = w2_ref.shape[0], w2_ref.shape[1]
-    planes = vox_ref.shape[0]
+    planes = PACK * halves
+    per = col_ref.shape[2] // x_ref.shape[1]
     wide = rows - planes
     kin = w1_ref.shape[1]
     chans = col_ref.shape[1]
@@ -145,15 +204,21 @@
         colour = jnp.sum(weight, axis=0, keepdims=True)
         for p in range(planes):
             colour = colour + weight[p : p + 1] * rad_ref[pl.ds(p * chans, chans), here]
-        col_ref[0, :, here] = colour
-        last_ref[0, :, here] = jnp.exp(-upto[planes - 1 : planes])
+        at = pl.multiple_of(lax.rem(step, per) * x_ref.shape[1] + c * sub, TILE)
+        col_ref[step // per, :, pl.ds(at, sub)] = colour
+        mine[step // per, 0:1, pl.ds(at, sub)] = jnp.exp(-upto[planes - 1 : planes])
+
+    @pl.when(step == steps - 1)
+    def _():
+        to_partner().wait()
+        share_state(n, me, col_ref, cots, cots_ref, state_ref, mine, got, back, land, s1, r1, s2, r2)
 
 
 def backward_kernel(
     dscale,
     sub,
     off_ref,
-    vox_ref,
+    x_ref,
     w1_ref,
     w1t_ref,
     w2_ref,
@@ -163,7 +228,6 @@
     gvox_ref,
     acc1_ref,
     acc2_ref,
-    x_ref,
     slope_ref,
     hid_ref,
     s_ref,
@@ -177,9 +241,8 @@
         acc1_ref[...] = jnp.zeros_like(acc1_ref)
         acc2_ref[...] = jnp.zeros_like(acc2_ref)
 
-    gather_tiles(off_ref, vox_ref, x_ref, step)
     halves, rows = w2_ref.shape[0], w2_ref.shape[1]
-    planes, feats, rays = vox_ref.shape
+    planes, feats, rays = gvox_ref.shape
     wide = rows - planes
     kin = w1_ref.shape[1]
     kmid = w1_ref.shape[0]
@@ -276,16 +339,16 @@
     return copies
 
 
-def state_kernel(n, last_ref, col_ref, cot_ref, out_ref, mine, got, back, s1, r1, s2, r2):
-    me = lax.axis_index("depth")
-    greet(n, me)
-
-    def fill(d, carry):
-        mine[d, 0:1, :] = last_ref[d]
-        mine[d, 1:2, :] = jnp.sum(col_ref[d] * cot_ref[d].astype(F32), axis=0, keepdims=True)
+def share_state(n, me, col_ref, cots, cots_ref, state_ref, mine, got, back, land, s1, r1, s2, r2):
+    def fill(q, carry):
+        for core in range(2):
+            cot = cots[q, core]
+            cots_ref[q, core] = cot
+            d = 2 * q + core
+            mine[d, 1:2, :] = jnp.sum(col_ref[d] * cot.astype(F32), axis=0, keepdims=True)
         return carry
 
-    lax.fori_loop(0, n, fill, 0)
+    lax.fori_loop(0, n // 2, fill, 0)
     copies = swap(n, me, lambda to: mine.at[to], got, s1, r1)
     got[me] = mine[me]
     for copy in copies:
@@ -299,25 +362,11 @@
         enter = enter * got[d, 0:1, :]
     for d in range(n):
         back[d, 1:2, :] = prior - back[d, 1:2, :]
-    copies = swap(n, me, lambda to: back.at[to], out_ref, s2, r2)
-    out_ref[me] = back[me]
+    copies = swap(n, me, lambda to: back.at[to], land, s2, r2)
+    land[me] = back[me]
     for copy in copies:
         copy.wait()
-
-
-def exchange_state(n, last, colour, cot):
-    chunk = last.shape[2]
-    shape = (n, 2, chunk)
-    vmem = pl.BlockSpec(memory_space=pltpu.VMEM)
-    return pl.pallas_call(
-        functools.partial(state_kernel, n),
-        out_shape=jax.ShapeDtypeStruct(shape, F32),
-        in_specs=[vmem] * 3,
-        out_specs=vmem,
-        scratch_shapes=[pltpu.VMEM(shape, F32)] * 3 + [pltpu.SemaphoreType.DMA((n,))] * 4,
-        compiler_params=pltpu.CompilerParams(collective_id=1, has_side_effects=True),
-        name="exchange_state",
-    )(last, colour, cot)
+    state_ref[...] = land[...]
 
 
 def total_kernel(n, a1_ref, a2_ref, g1_ref, g2_ref, give, got, mine, full, s1, r1, s2, r2):
@@ -397,7 +446,6 @@
     block = min(BLOCK, chunk)
     per = chunk // block
     steps = rays // block
-    cot = lax.all_gather(cotangent.astype(BF), "depth")
 
     smem = pl.BlockSpec(memory_space=pltpu.SMEM)
     vmem = pl.BlockSpec(memory_space=pltpu.VMEM)
@@ -413,27 +461,38 @@
         jax.ShapeDtypeStruct((halves, rows, PACK * hid), BF),
         jax.ShapeDtypeStruct((halves, PACK * hid, rows), BF),
     )
-    colour, last, *weights = pl.pallas_call(
+    x_spec = pl.BlockSpec((planes * feats, block), lambda i: (0, i))
+    sheared = shear(offsets, voxels)
+    halved = (n // 2, 2, chans, chunk)
+    pair = (n, 2, chunk)
+    colour, cot, state, *weights = pl.pallas_call(
         functools.partial(forward_kernel, dscale, min(FSUB, block)),
         grid=(steps,),
         out_shape=(
             jax.ShapeDtypeStruct((n, chans, chunk), F32),
-            jax.ShapeDtypeStruct((n, 1, chunk), F32),
+            jax.ShapeDtypeStruct(halved, BF),
+            jax.ShapeDtypeStruct(pair, F32),
         )
         + weights,
-        in_specs=[smem] + [vmem] * 3,
-        out_specs=(ray_spec(chans), ray_spec(1)) + (vmem,) * 4,
+        in_specs=[x_spec] + [vmem] * 3,
+        out_specs=(vmem,) * 7,
         scratch_shapes=[
-            pltpu.VMEM((planes * feats, block), BF),
             pltpu.VMEM((planes * chans, block), F32),
-        ],
-        compiler_params=params,
+            pltpu.VMEM(halved, BF),
+        ]
+        + [pltpu.VMEM(pair, F32)] * 4
+        + [pltpu.SemaphoreType.DMA((n // 2,))] * 2
+        + [pltpu.SemaphoreType.DMA] * 2
+        + [pltpu.SemaphoreType.DMA((n,))] * 4,
+        compiler_params=pltpu.CompilerParams(
+            vmem_limit_bytes=60 * 2**20, collective_id=1, has_side_effects=True
+        ),
         cost_estimate=pl.CostEstimate(
             flops=8 * 10**9, bytes_accessed=12 * 2**20, transcendentals=10**7
         ),
         name="forward",
-    )(offsets, voxels, w_first, w_second)
-    state = exchange_state(n, last, colour, cot)
+    )(sheared, w_first, w_second, cotangent)
+    cot = cot.reshape(n, chans, chunk)
     share = (state[:, 0:1, :] * colour).astype(BF)
     image = lax.psum_scatter(share, "depth", scatter_dimension=0).astype(F32)
     gvox, acc1, acc2 = pl.pallas_call(
@@ -444,10 +503,9 @@
             jax.ShapeDtypeStruct((PACK * hid, PACK * feats), F32),
             jax.ShapeDtypeStruct((halves, rows, PACK * hid), F32),
         ),
-        in_specs=[smem] + [vmem] * 5 + [ray_spec(chans), ray_spec(2)],
+        in_specs=[smem, x_spec] + [vmem] * 4 + [ray_spec(chans), ray_spec(2)],
         out_specs=(vmem, vmem, vmem),
         scratch_shapes=[
-            pltpu.VMEM((planes * feats, block), BF),
             pltpu.VMEM((planes * hid, block), F32),
             pltpu.VMEM((planes * hid, block), BF),
             pltpu.VMEM((planes * chans, block), F32),
@@ -459,7 +517,7 @@
             flops=60 * 10**9, bytes_accessed=24 * 2**20, transcendentals=10**7
         ),
         name="backward",
-    )(offsets, voxels, *weights, cot, state)
+    )(offsets, sheared, *weights, cot, state)
     grad_first, grad_second = total_over_depth(n, acc1, acc2, w_first.shape, w_second.shape)
     return image, gvox, grad_first, grad_second
 

time: 142 us -> 131 us (0.923)
  waiting for transfers between devices: 19.1 us -> 0.02 us
  Pallas kernels: 99.1 us -> 106 us
    all_gather x1 -> x0, waiting for transfers between devices: 19.1 us -> none  [shards(): cot = lax.all_gather(cotangent.astype(BF), 'depth')]
    pallas_call x1, Pallas kernels: 21.5 us -> 36.7 us  [shards(): pl.pallas_call(functools.partial(forward_kernel, dscale, min(FSUB, block)...]
    pallas_call x1, Pallas kernels: 15.4 us -> 9.76 us  [shear(): pl.pallas_call(shear_kernel, grid=(planes,), out_shape=jax.ShapeDtypeStru...]
    pallas_call x1, Pallas kernels: 48.7 us -> 46.3 us  [shards(): pl.pallas_call(functools.partial(backward_kernel, dscale, min(BSUB, block...]
    convert_element_type x1, other arithmetic: 1.26 us -> 2.87 us  [shards(): share = (state[:, 0:1, :] * colour).astype(BF)]
    convert_element_type x1 -> x0, other arithmetic: 1.53 us -> none  [shards(): cot = lax.all_gather(cotangent.astype(BF), 'depth')]
    unnamed x6 -> x4, local copies, waits for them, and re-layouts: 4.18 us -> 4.17 us
  transfers between devices with their start and end apart: 2 -> 1, of which waited for: 1 -> 0; matrix products, arithmetic and copies ran while one was open for 2% -> 1% of each run, Pallas kernels for 59% -> 46%
where the time goes in v3:
time: 131 us; the launch traced here: 130 us
  Pallas kernels  106 us (81%)
  between operations  14.1 us (11%)
  local copies, waits for them, and re-layouts  5.12 us (4%)
  other arithmetic  4.37 us (3%)
    pallas_call x1, Pallas kernels, shards(): pl.pallas_call(functools.partial(backward_kernel, dscale, min(BSUB, block...  46.3 us
    pallas_call x1, Pallas kernels, shards(): pl.pallas_call(functools.partial(forward_kernel, dscale, min(FSUB, block)...  36.7 us
    pallas_call x1, Pallas kernels, total_over_depth(): pl.pallas_call(functools.partial(total_kernel, n), out_shape=(jax.ShapeDt...  13.7 us
    pallas_call x1, Pallas kernels, shear(): pl.pallas_call(shear_kernel, grid=(planes,), out_shape=jax.ShapeDtypeStru...  9.76 us
    unnamed x4, local copies, waits for them, and re-layouts  4.17 us
    convert_element_type x1, other arithmetic, shards(): share = (state[:, 0:1, :] * colour).astype(BF)  2.87 us
  transfers between devices with their start and end apart: 1, of which 0 were waited for; matrix products, arithmetic and copies ran while one was open for 1% of the time, Pallas kernels for 46%

profile of v3, /device:TPU:0, one launch (start us, length us, event | category | flops | bytes accessed | tf_op | source)
XLA Modules:
  0.0 130.1 jit_solution(5585575174043918838)
XLA Ops:
  7.2 0.0 reduce-scatter.2.cloned.1.call-start
  7.2 1.4 %copy.9.first_ref = bf16[64,32]{1,0:T(8,128)(2,1)} copy(bf16[64,32]{0,1:T(8,128)(2,1)} %param.7) | data formatting | bytes 8192 | tf_op args[2]
  8.6 9.8 %shear.1.x_ref = bf16[256,16384]{1,0:T(8,128)(2,1)} custom-call(s32[128]{0:T(128)} %off_ref.3, bf16[8,32,16384]{2,1,0:T(8,128)(2,1)} %vox_ref.1), custom_call_target="tpu_custom_call" | custom-call | tf_op jit(solution)/shard_map/shear/pallas_call | solution.py:58
  18.4 36.7 %forward.1 = (f32[16,32,1024]{2,1,0:T(8,128)}, bf16[8,2,32,1024]{3,2,1,0:T(8,128)(2,1)}, f32[16,2,1024]{2,1,0:T(2,128)}, bf16[256,128]{1,0:T(8,128)(2,1)}, bf16[...) custom-call(bf16[256,16384]{1,0:T(8,128)(2,1)} %shear.1.x_ref, ...), custom_call_target="tpu_custom_call" | custom-call | flops 8000000000 | bytes 12582912 | tf_op jit(solution)/shard_map/forward/pallas_call | solution.py:468
  55.1 1.0 slice.3
  56.1 2.9 %multiply_convert_fusion = bf16[16,32,1024]{2,1,0:T(8,128)(2,1)} fusion(f32[16,32,1024]{2,1,0:T(8,128)} %get-tuple-element.17, f32[16,1024]{1,0:T(8,128)S(1)} %bitcast.7), kind=kLoop, calls=%fused_computation | loop fusion | flops 1048576 | bytes 3211264 | tf_op jit(solution)/shard_map/convert_element_type | solution.py:496
  58.9 0.0 reduce-scatter.2.cloned.1.call-update
  59.0 46.3 %backward.1 = (bf16[8,32,16384]{2,1,0:T(8,128)(2,1)}, f32[256,128]{1,0:T(8,128)}, f32[2,136,256]{2,1,0:T(8,128)}) custom-call(s32[128]{0:T(128)} %off_ref.3, bf16[256,16384]{1,0:T(8,128)(2,1)} %shear.1.x_ref, bf16[256,128]{1,0:T(8,128)(2,1)} %get-tuple-element.18.w1_ref, bf16[128,256]{1,0:T(8,128)(2,1)} %get-tuple-element.19.w1t_ref, ...), custom_call_target="tpu_custom_call" | custom-call | flops 60000002048 | bytes 25165824 | tf_op jit(solution)/shard_map/backward/pallas_call | solution.py:498
  105.3 13.7 %total_over_depth.1 = (f32[64,32]{1,0:T(8,128)}, f32[33,64]{1,0:T(8,128)}) custom-call(f32[256,128]{1,0:T(8,128)} %get-tuple-element.24.a1_ref, f32[2,136,256]{2,1,0:T(8,128)} %get-tuple-element.25.a2_ref), custom_call_target="tpu_custom_call" | custom-call | tf_op jit(solution)/shard_map/total_over_depth/pallas_call | solution.py:422
  119.0 1.4 %copy.10 = f32[64,32]{0,1:T(8,128)} copy(f32[64,32]{1,0:T(8,128)} %get-tuple-element.30) | data formatting | bytes 16384
  120.4 0.0 reduce-scatter.2.cloned.1.call-done
  120.4 1.5 %bitcast_convert_fusion = f32[32,1024]{1,0:T(8,128)} fusion(bf16[1,32,1024]{2,1,0:T(8,128)(2,1)} %reduce-scatter.2.cloned.1.call-done), kind=kLoop, calls=%fused_computation.2 | loop fusion | flops 32768 | bytes 196608 | tf_op jit(solution)/shard_map/convert_element_type | solution.py:497
  121.9 1.3 %copy.15 = f32[33,64]{1,0:T(8,128)} copy(f32[33,64]{1,0:T(8,128)} %get-tuple-element.39) | data formatting | bytes 16896
  (1 shorter events, 0.0 us)
Async XLA Ops:
  7.2 113.2 %reduce-scatter.2.cloned.1.call-start = ((), (), s32[]{:S(2)}) async-start(), calls=%async_computation.1 | async-start | bytes 1114112 | tf_op jit(solution)/shard_map/reduce_scatter | solution.py:497
Sparse Core Ops, SparseCore 0:
  59.1 57.5 reduce-scatter.1
